TPU v7x, 32 devices: a whole 2x2x4 slice. The times are simulated.
32 devices in a mesh: groups: 2 (over y), tm: 8 (over z, x), height: 2 (over core).
Axes of the slice: x: 2, y: 2, z: 4, core: 2. Of those that a mesh axis runs over, the one named last changes fastest.
Arguments:
- video: bfloat16 [32, 8, 64, 256], P(('groups', 'tm'), 'height'), parts along dimension 0, may hold values from -6 to 6
- block_ids: int32 [32], P('groups'), parts along dimension 0, may hold values from 0 to 4, never falling along the last dimension, each value on 1 to 4 neighbouring positions
- conv_weight: bfloat16 [3, 3, 3, 256, 256], replicated, may hold values from -0.078125 to 0.078125
- w_query: bfloat16 [256, 256], replicated, may hold values from -4 to 4
- w_key: bfloat16 [256, 256], replicated, may hold values from -4 to 4
- w_value: bfloat16 [256, 256], replicated, may hold values from -0.375 to 0.375
- w_output: bfloat16 [256, 256], replicated, may hold values from -0.375 to 0.375
Outputs:
- encoded: bfloat16 [32, 8, 64, 256], P(('groups', 'tm'), 'height'), parts along dimension 0
There are 2 independent parts, one for each index of `groups`. A program takes and returns all parts, laid end to end along the dimension named above; an argument that names none is the same for every part. Nothing has to cross between parts.
Inputs may be any that keep to these rules, and one draw needn't show every extreme that they name: `block_ids`: block ids never fall along the frames and start at 0; each block has 1 to 4 frames, and some block has exactly 4.
All inputs are finite; a program needn't handle non-finite values.
Results may differ from a plain program's by a relative error of at most 0.012.
Values may be sent and summed in bfloat16 or wider, within the bound.
A program may use at most 64 MiB of HBM per device.

v0:
```python
import jax
import jax.numpy as jnp
from jax import lax
from jax.sharding import PartitionSpec as P

HD = 64


def passed_along(value, axis, by):
    count = lax.axis_size(axis)
    pairs = [(i, i + by) for i in range(count) if 0 <= i + by < count]
    return lax.ppermute(value, axis, pairs)


def with_halo(value, sides, width):
    for axis, dim in sides:
        count, length = (lax.axis_size(axis), value.shape[dim])
        up = [(i, (i + 1) % count) for i in range(count - 1)]
        down = [(j, i) for i, j in up]
        last = lax.slice_in_dim(value, length - width, length, axis=dim)
        first = lax.slice_in_dim(value, 0, width, axis=dim)
        before = lax.ppermute(last, axis, up)
        after = lax.ppermute(first, axis, down)
        value = jnp.concatenate([before, value, after], axis=dim)
    return value


def normalize(values):
    wide = values.astype(jnp.float32)
    return wide * lax.rsqrt(jnp.mean(wide * wide, axis=-1, keepdims=True) + 1e-06)


def project(flat, weight):
    return jnp.dot(flat, weight, preferred_element_type=jnp.float32).astype(jnp.bfloat16)


def per_device(video, block_ids, conv_weight, w_query, w_key, w_value, w_output):
    count, rows, cols, chans = video.shape
    heads = chans // HD
    activated = jax.nn.silu(normalize(video)).astype(jnp.bfloat16)
    cached = passed_along(activated, "tm", 1)
    extended = jnp.concatenate([cached, activated], axis=0)
    rimmed = with_halo(extended, (("height", 1),), 1)
    padded = jnp.pad(rimmed, ((0, 0), (0, 0), (1, 1), (0, 0)))
    total = jnp.zeros((count * rows * cols, chans), jnp.float32)
    for tap_t in range(3):
        for tap_r in range(3):
            for tap_w in range(3):
                window = padded[
                    tap_t : tap_t + count, tap_r : tap_r + rows, tap_w : tap_w + cols
                ].reshape(-1, chans)
                total = total + jnp.dot(
                    window, conv_weight[tap_t, tap_r, tap_w], preferred_element_type=jnp.float32
                )
    hidden = (video.astype(jnp.float32) + total.reshape(video.shape)).astype(jnp.bfloat16)
    normed = normalize(hidden).astype(jnp.bfloat16).reshape(-1, chans)
    pixels = rows * cols
    tm_count = lax.axis_size("tm")
    per_dev = -(-pixels // tm_count)
    padded_pix = per_dev * tm_count
    grid = normed.reshape(count, pixels, chans)
    grid = grid.reshape(count, tm_count, per_dev, chans)
    piece = lax.all_to_all(grid, "tm", split_axis=1, concat_axis=0, tiled=True)
    frames_all = piece.shape[0]
    several = piece.shape[2]
    flat = piece.reshape(-1, chans)
    query_p = project(flat, w_query).reshape(frames_all, several, heads, HD)
    keys_p = project(flat, w_key).reshape(frames_all, several, heads, HD)
    vals_p = project(flat, w_value).reshape(frames_all, several, heads, HD)
    order = jnp.arange(frames_all, dtype=jnp.int32)
    permit = (order[None, :] <= order[:, None]) & (block_ids[None, :] >= block_ids[:, None] - 1)
    scores_p = jnp.einsum(
        "fphd,kphd->phfk", query_p, keys_p, preferred_element_type=jnp.float32
    ) * HD ** (-0.5)
    scores_p = jnp.where(permit[None, None], scores_p, -1e30)
    top_p = jnp.max(scores_p, axis=-1, keepdims=True)
    expo_p = jnp.exp(scores_p - top_p)
    weights_p = (expo_p / jnp.sum(expo_p, axis=-1, keepdims=True)).astype(jnp.bfloat16)
    result = jnp.einsum("phfk,kphd->fphd", weights_p, vals_p, preferred_element_type=jnp.float32)
    gone = result.astype(jnp.bfloat16).reshape(frames_all, 1, several, chans)
    back = lax.all_to_all(gone, "tm", split_axis=0, concat_axis=1, tiled=True)
    attended = back.reshape(count, padded_pix, chans).reshape(-1, chans)
    mixed = hidden.astype(jnp.float32).reshape(-1, chans) + jnp.dot(
        attended, w_output, preferred_element_type=jnp.float32
    )
    return mixed.astype(jnp.bfloat16).reshape(video.shape)


def solution(mesh):
    placed = (P(("groups", "tm"), "height", None, None), P("groups"), P(), P(), P(), P(), P())
    return jax.shard_map(
        per_device,
        mesh=mesh,
        in_specs=placed,
        out_specs=P(("groups", "tm"), "height", None, None),
        check_vma=False,
    )
```

profile of v0, /device:TPU:0, one launch (start us, length us, event | category | flops | bytes accessed | tf_op | source)
XLA Modules:
  0.0 62.3 jit_solution(18016009349427102440)
XLA Ops:
  0.0 1.1 %fusion.18 = f32[2,4,64]{2,1,0:T(4,128)S(1)} fusion(bf16[2,4,64,256]{3,2,1,0:T(8,128)(2,1)} %param.7), kind=kLoop, calls=%fused_computation.58 | loop fusion | flops 392704 | bytes 264192 | tf_op jit(solution)/shard_map/reduce_sum | solution.py:30
  1.1 1.2 %fusion.17 = bf16[2,4,64,256]{3,2,1,0:T(8,128)(2,1)S(1)} fusion(bf16[2,4,64,256]{3,2,1,0:T(8,128)(2,1)} %param.7, f32[2,4,64]{2,1,0:T(4,128)S(1)} %add_rsqrt_fusion.1), kind=kLoop, calls=%fused_computation.57 | loop fusion | flops 917504 | bytes 526336 | tf_op jit(solution)/shard_map/convert_element_type | solution.py:40
  2.3 4.9 %collective-permute-start = (bf16[2,4,64,256]{3,2,1,0:T(8,128)(2,1)S(1)}, bf16[2,4,64,256]{3,2,1,0:T(8,128)(2,1)S(1)}, u32[]{:S(2)}, u32[]{:S(2)}) collective-permute-start(bf16[2,4,64,256]{3,2,1,0:T(8,128)(2,1)S(1)} %fusion.17), channel_id=1, source_target_pairs={{0,2},{2,4},{4,6},{6,8},{8,10},{10,12},{12,14},{1,3},{3,5},{5,7},{... | collective-permute-start | bytes 786440 | tf_op jit(solution)/shard_map/ppermute | solution.py:12
  7.2 5.5 %collective-permute-done = bf16[2,4,64,256]{3,2,1,0:T(8,128)(2,1)S(1)} collective-permute-done((bf16[2,4,64,256]{3,2,1,0:T(8,128)(2,1)S(1)}, bf16[2,4,64,256]{3,2,1,0:T(8,128)(2,1)S(1)}, u32[]{:S(2)}, u32[]{:S(2)}) %collective-permute-start) | collective-permute-done | bytes 262176 | tf_op jit(solution)/shard_map/ppermute | solution.py:12
  12.8 1.3 %collective-permute-start.1 = (bf16[4,1,64,256]{3,2,1,0:T(8,128)(2,1)S(1)}, bf16[4,1,64,256]{3,2,1,0:T(8,128)(2,1)S(1)}, u32[]{:S(2)}, u32[]{:S(2)}) collective-permute-start(bf16[4,1,64,256]{3,2,1,0:T(8,128)(2,1)S(1)} %get-tuple-element.33), channel_id=1, source_target_pairs={{0,1},{2,3},{4,5},{6,7},{8,9},{10,11},{12,13},{14,15},{16,17},{18,... | collective-permute-start | bytes 393224 | tf_op jit(solution)/shard_map/ppermute | solution.py:22
  14.1 1.3 %collective-permute-start.2 = (bf16[4,1,64,256]{3,2,1,0:T(8,128)(2,1)S(1)}, bf16[4,1,64,256]{3,2,1,0:T(8,128)(2,1)S(1)}, u32[]{:S(2)}, u32[]{:S(2)}) collective-permute-start(bf16[4,1,64,256]{3,2,1,0:T(8,128)(2,1)S(1)} %get-tuple-element.34), channel_id=1, source_target_pairs={{1,0},{3,2},{5,4},{7,6},{9,8},{11,10},{13,12},{15,14},{17,16},{19,... | collective-permute-start | bytes 393224 | tf_op jit(solution)/shard_map/ppermute | solution.py:23
  15.4 1.9 %collective-permute-done.2 = bf16[4,1,64,256]{3,2,1,0:T(8,128)(2,1)S(1)} collective-permute-done((bf16[4,1,64,256]{3,2,1,0:T(8,128)(2,1)S(1)}, bf16[4,1,64,256]{3,2,1,0:T(8,128)(2,1)S(1)}, u32[]{:S(2)}, u32[]{:S(2)}) %collective-permute-start.2) | collective-permute-done | bytes 131104 | tf_op jit(solution)/shard_map/ppermute | solution.py:23
  17.3 0.5 select_maximum_fusion
  17.8 0.8 %fusion.84 = (bf16[2,4,64,256]{3,2,1,0:T(8,128)(2,1)S(1)}, bf16[2,4,64,256]{3,2,1,0:T(8,128)(2,1)S(1)}, bf16[2,4,64,256]{3,2,1,0:T(8,128)(2,1)S(1)}, bf16[2,4,64...) fusion(bf16[4,6,66,256]{3,2,1,0:T(8,128)(2,1)S(1)} %select_maxi, ...), kind=kLoop, calls=%fused_computation.132 | loop fusion | bytes 9437184 | tf_op jit(solution)/shard_map/slice | solution.py:49
  18.7 1.2 %copy-done.1 = bf16[3,3,3,256,256]{4,3,2,1,0:T(8,128)(2,1)S(1)} copy-done((bf16[3,3,3,256,256]{4,3,2,1,0:T(8,128)(2,1)S(1)}, bf16[3,3,3,256,256]{4,3,2,1,0:T(8,128)(2,1)}, u32[]{:S(2)}) %copy-start.1) | copy-done | bytes 3538968
  21.5 0.2 fusion.7
  23.3 0.2 fusion.6
  26.8 0.7 %copy.32 = bf16[2,8,32,256]{3,2,0,1:T(8,128)(2,1)} copy(bf16[2,8,32,256]{3,2,1,0:T(8,128)(2,1)S(1)} %bitcast.170) | data formatting | bytes 524288 | tf_op jit(solution)/shard_map/reshape;reshape;reshape | solution.py:62
  27.5 6.8 %all-to-all-start = ((bf16[2,8,32,256]{3,2,0,1:T(8,128)(2,1)}), bf16[2,8,32,256]{3,2,0,1:T(8,128)(2,1)S(1)}, u32[]{:S(2)}, u32[]{:S(2)}) async-start(bf16[2,8,32,256]{3,2,0,1:T(8,128)(2,1)} %copy.32), calls=%async_computation | async-start | bytes 524288 | tf_op jit(solution)/shard_map/all_to_all | solution.py:63
  34.4 9.1 %all-to-all-done = bf16[2,8,32,256]{3,2,0,1:T(8,128)(2,1)S(1)} async-done(((bf16[2,8,32,256]{3,2,0,1:T(8,128)(2,1)}), bf16[2,8,32,256]{3,2,0,1:T(8,128)(2,1)S(1)}, u32[]{:S(2)}, u32[]{:S(2)}) %all-to-all-start) | async-done | bytes 262176 | tf_op jit(solution)/shard_map/all_to_all | solution.py:63
  43.7 0.2 reshape.197
  44.2 0.2 reshape.198
  44.7 0.2 reshape.196
  45.0 2.0 %fusion.87 = (f32[32,4,16]{2,1,0:T(4,128)S(1)}, f32[32,4,16,16]{2,3,1,0:T(8,128)}) fusion(bf16[16,32,4,64]{3,2,1,0:T(4,128)(2,1)S(1)} %reshape.198, bf16[16,32,4,64]{3,2,1,0:T(4,128)(2,1)S(1)} %reshape.197, pred[16,16]{0,1:T(8,128)(4,1)S(1)} %fusion.82), kind=kOutput, calls=%fused_computation.135 | convolution fusion | flops 4325391 | bytes 663808 | tf_op jit(solution)/shard_map/sub | solution.py:77
  47.0 1.8 %fusion.5 = bf16[16,32,4,64]{3,0,2,1:T(8,128)(2,1)S(1)} fusion(f32[32,4,16,16]{2,3,1,0:T(8,128)} %get-tuple-element.36, bf16[16,32,4,64]{3,2,1,0:T(4,128)(2,1)S(1)} %reshape.196, f32[32,4,16]{2,1,0:T(4,128)S(1)} %get-tuple-element.35), kind=kOutput, calls=%fused_computation.9 | convolution fusion | flops 4390912 | bytes 663552 | tf_op jit(solution)/shard_map/phfk,kphd->fphd/dot_general | solution.py:79
  48.7 0.3 copy.37
  49.0 0.3 reshape.199
  49.4 11.9 %all_to_all.30 = bf16[16,1,32,256]{3,2,1,0:T(8,128)(2,1)S(1)} all-to-all(bf16[16,1,32,256]{3,2,1,0:T(8,128)(2,1)S(1)} %bitcast.171), channel_id=1, replica_groups=mesh['groups'=2,'tm'=8,'height'=2] {'tm'}, dimensions={0} | all-to-all | bytes 524288 | tf_op jit(solution)/shard_map/all_to_all | solution.py:81
  61.3 0.9 %fusion.8 = bf16[512,256]{1,0:T(8,128)(2,1)} fusion(f32[512,256]{1,0:T(8,128)S(1)} %bitcast.161, bf16[512,256]{1,0:T(8,128)(2,1)S(1)} %bitcast.194, bf16[256,256]{1,0:T(8,128)(2,1)S(1)} %copy-done.5), kind=kOutput, calls=%fused_computation.40 | convolution fusion | flops 67371008 | bytes 1179648 | tf_op jit(solution)/shard_map/dot_general | solution.py:83
  (53 shorter events, 7.1 us)
Async XLA Ops:
  0.0 43.5 %copy-start = (bf16[256,256]{1,0:T(8,128)(2,1)S(1)}, bf16[256,256]{1,0:T(8,128)(2,1)}, u32[]{:S(2)}) copy-start(bf16[256,256]{1,0:T(8,128)(2,1)} %param.10) | copy-start | bytes 393220
  2.3 10.4 %collective-permute-start = (bf16[2,4,64,256]{3,2,1,0:T(8,128)(2,1)S(1)}, bf16[2,4,64,256]{3,2,1,0:T(8,128)(2,1)S(1)}, u32[]{:S(2)}, u32[]{:S(2)}) collective-permute-start(bf16[2,4,64,256]{3,2,1,0:T(8,128)(2,1)S(1)} %fusion.17), channel_id=1, source_target_pairs={{0,2},{2,4},{4,6},{6,8},{8,10},{10,12},{12,14},{1,3},{3,5},{5,7},{... | collective-permute-start | bytes 786440 | tf_op jit(solution)/shard_map/ppermute | solution.py:12
  12.8 2.6 %collective-permute-start.1 = (bf16[4,1,64,256]{3,2,1,0:T(8,128)(2,1)S(1)}, bf16[4,1,64,256]{3,2,1,0:T(8,128)(2,1)S(1)}, u32[]{:S(2)}, u32[]{:S(2)}) collective-permute-start(bf16[4,1,64,256]{3,2,1,0:T(8,128)(2,1)S(1)} %get-tuple-element.33), channel_id=1, source_target_pairs={{0,1},{2,3},{4,5},{6,7},{8,9},{10,11},{12,13},{14,15},{16,17},{18,... | collective-permute-start | bytes 393224 | tf_op jit(solution)/shard_map/ppermute | solution.py:22
  14.1 3.2 %collective-permute-start.2 = (bf16[4,1,64,256]{3,2,1,0:T(8,128)(2,1)S(1)}, bf16[4,1,64,256]{3,2,1,0:T(8,128)(2,1)S(1)}, u32[]{:S(2)}, u32[]{:S(2)}) collective-permute-start(bf16[4,1,64,256]{3,2,1,0:T(8,128)(2,1)S(1)} %get-tuple-element.34), channel_id=1, source_target_pairs={{1,0},{3,2},{5,4},{7,6},{9,8},{11,10},{13,12},{15,14},{17,16},{19,... | collective-permute-start | bytes 393224 | tf_op jit(solution)/shard_map/ppermute | solution.py:23
  17.8 2.0 %copy-start.1 = (bf16[3,3,3,256,256]{4,3,2,1,0:T(8,128)(2,1)S(1)}, bf16[3,3,3,256,256]{4,3,2,1,0:T(8,128)(2,1)}, u32[]{:S(2)}) copy-start(bf16[3,3,3,256,256]{4,3,2,1,0:T(8,128)(2,1)} %param.9) | copy-start | bytes 10616836
  25.2 1.2 %copy-start.2 = (bf16[2,4,64,256]{3,2,1,0:T(8,128)(2,1)S(1)}, bf16[2,4,64,256]{3,2,1,0:T(8,128)(2,1)}, u32[]{:S(2)}) copy-start(bf16[2,4,64,256]{3,2,1,0:T(8,128)(2,1)} %param.7) | copy-start | bytes 786436
  25.7 8.6 %copy-start.6 = (s32[16]{0:T(128)S(1)}, s32[16]{0:T(128)}, u32[]{:S(2)}) copy-start(s32[16]{0:T(128)} %param.8) | copy-start | bytes 196
  25.9 18.0 %copy-start.3 = (bf16[256,256]{1,0:T(8,128)(2,1)S(1)}, bf16[256,256]{1,0:T(8,128)(2,1)}, u32[]{:S(2)}) copy-start(bf16[256,256]{1,0:T(8,128)(2,1)} %param.11) | copy-start | bytes 393220
  26.2 18.3 %copy-start.4 = (bf16[256,256]{1,0:T(8,128)(2,1)S(1)}, bf16[256,256]{1,0:T(8,128)(2,1)}, u32[]{:S(2)}) copy-start(bf16[256,256]{1,0:T(8,128)(2,1)} %param.12) | copy-start | bytes 393220
  27.5 16.0 %all-to-all-start = ((bf16[2,8,32,256]{3,2,0,1:T(8,128)(2,1)}), bf16[2,8,32,256]{3,2,0,1:T(8,128)(2,1)S(1)}, u32[]{:S(2)}, u32[]{:S(2)}) async-start(bf16[2,8,32,256]{3,2,0,1:T(8,128)(2,1)} %copy.32), calls=%async_computation | async-start | bytes 524288 | tf_op jit(solution)/shard_map/all_to_all | solution.py:63
  47.0 14.3 %copy-start.5 = (bf16[256,256]{1,0:T(8,128)(2,1)S(1)}, bf16[256,256]{1,0:T(8,128)(2,1)}, u32[]{:S(2)}) copy-start(bf16[256,256]{1,0:T(8,128)(2,1)} %param.13) | copy-start | bytes 393220
where the time goes:
time: 62.7 us; the launch traced here: 62.3 us
  waiting for transfers between devices  16.6 us (26%)
  starting transfers between devices  14.3 us (23%)
  blocking collectives  11.9 us (19%)
  matrix products  11.5 us (18%)
  local copies, waits for them, and re-layouts  4.25 us (7%)
  other arithmetic  3.32 us (5%)
    all_to_all x1, blocking collectives, per_device(): back = lax.all_to_all(gone, 'tm', split_axis=0, concat_axis=1, tiled=True)  11.9 us
    all_to_all x1, waiting for transfers between devices, per_device(): piece = lax.all_to_all(grid, 'tm', split_axis=1, concat_axis=0, tiled=True)  9.14 us
    all_to_all x1, starting transfers between devices, per_device(): piece = lax.all_to_all(grid, 'tm', split_axis=1, concat_axis=0, tiled=True)  6.79 us
    dot_general x27, matrix products, per_device(): jnp.dot(window, conv_weight[tap_t, tap_r, tap_w], preferred_element_type=...  6.11 us
    ppermute x1, waiting for transfers between devices, passed_along(): return lax.ppermute(value, axis, pairs)  5.53 us
    ppermute x1, starting transfers between devices, passed_along(): return lax.ppermute(value, axis, pairs)  4.89 us
    sub x1, matrix products, per_device(): expo_p = jnp.exp(scores_p - top_p)  2 us
    ppermute x1, waiting for transfers between devices, with_halo(): after = lax.ppermute(first, axis, down)  1.9 us
  transfers between devices with their start and end apart: 4, of which 3 were waited for; matrix products, arithmetic and copies ran while one was open for 0% of the time, Pallas kernels for 0%

commit v1 on v0

v1 whole, which is shorter than its diff:
```python
import functools

import jax
import jax.numpy as jnp
from jax import lax
from jax.experimental import pallas as pl
from jax.experimental.pallas import tpu as pltpu
from jax.sharding import PartitionSpec as P

HD = 64
REACH = 7
MESH = pl.DeviceIdType.MESH


def normalize(wide):
    return wide * lax.rsqrt(jnp.mean(wide * wide, axis=-1, keepdims=True) + 1e-06)


def kernel(n, parts, ids, video, conv_w, w_q, w_k, w_v, w_o, out,
           raw, act, cw, pw, acc, held, nb, qs, ks, vs, place, spread,
           load_sem, weight_sem, row_send, row_recv, halo_send, halo_recv,
           own_send, fwd_send, nb_recv):
    count, rows, cols, chans = video.shape
    pix = rows * cols
    heads = chans // HD
    me = lax.axis_index("tm")
    core = lax.axis_index("height")
    even = lax.rem(me, 2) == 0
    odd = lax.rem(me, 2) == 1
    chunk = pix // parts

    def peer(by):
        return {"tm": me + by}

    other = {"height": 1 - core}

    own_load = pltpu.make_async_copy(video, raw.at[2:4, 1:rows + 1], load_sem)
    own_load.start()
    w_loads = {}
    for a in (2, 1, 0):
        w_loads[a] = pltpu.make_async_copy(conv_w.at[a], cw.at[a], weight_sem.at[a])
        w_loads[a].start()
    p_loads = []
    for j, w in enumerate((w_q, w_k, w_v, w_o)):
        p_loads.append(pltpu.make_async_copy(w, pw.at[j], weight_sem.at[3 + j]))
        p_loads[-1].start()

    barrier = pltpu.get_barrier_semaphore()
    near = [(me >= 1, -1), (me <= n - 2, 1), (me >= 2, -2), (me <= n - 3, 2)]
    pl.semaphore_signal(barrier, inc=1, device_id=other, device_id_type=MESH)
    for cond, by in near:
        @pl.when(cond)
        def _(by=by):
            pl.semaphore_signal(barrier, inc=1, device_id=peer(by), device_id_type=MESH)

    blank = jnp.zeros((cols, chans), jnp.bfloat16)
    outer = (rows + 1) * core
    inner = (rows + 1) * (1 - core)
    for e in range(4):
        raw[e, outer] = blank

    @pl.when(me == 0)
    def _():
        for e in range(2):
            for r in range(rows + 2):
                raw[e, r] = blank

    for d in range(1, 5):
        @pl.when(me < d)
        def _(d=d):
            for f in range(2):
                nb[8 - 2 * d + f] = jnp.zeros((pix, chans), jnp.bfloat16)

    for at in (0, 1, n - 2, n - 1):
        @pl.when(me == at)
        def _(at=at):
            pl.semaphore_wait(barrier, 1 + sum(0 <= at + by < n for by in (-2, -1, 1, 2)))

    @pl.when((me >= 2) & (me <= n - 3))
    def _():
        pl.semaphore_wait(barrier, 5)

    edge = (rows - 1) * (1 - core)
    landing = (rows + 1) * core

    def halo(f):
        return pltpu.make_async_remote_copy(
            src_ref=video.at[f], dst_ref=raw.at[f, 1:rows + 1],
            send_sem=halo_send.at[f], recv_sem=halo_recv.at[f],
            device_id=peer(1), device_id_type=MESH)

    def row(e):
        src = video.at[e - 2, edge] if e >= 2 else raw.at[e, 1 + edge]
        return pltpu.make_async_remote_copy(
            src_ref=src, dst_ref=raw.at[e, landing],
            send_sem=row_send.at[e], recv_sem=row_recv.at[e],
            device_id=other, device_id_type=MESH)

    @pl.when(me <= n - 2)
    def _():
        halo(1).start()
        halo(0).start()

    row(2).start()
    row(3).start()

    for f in range(2):
        for s in range(f, f + 8):
            c0 = lax.broadcasted_iota(jnp.int32, (chans, 128), 0) // HD
            l0 = lax.broadcasted_iota(jnp.int32, (chans, 128), 1)
            place[f * 8 + s - f] = jnp.where(
                l0 == c0 + (s * 8 + f * 4), HD ** (-0.5), 0.0).astype(jnp.bfloat16)
            c1 = lax.broadcasted_iota(jnp.int32, (128, chans), 1) // HD
            l1 = lax.broadcasted_iota(jnp.int32, (128, chans), 0)
            spread[f * 8 + s - f] = jnp.where(
                l1 == c1 + (s * 8 + f * 4), 1.0, 0.0).astype(jnp.bfloat16)

    col = lax.broadcasted_iota(jnp.int32, (cols, chans), 0)

    def activate(e, r):
        v = normalize(raw[e, r].astype(jnp.float32))
        v = v / (1.0 + jnp.exp(-v))
        act[e, r, :, chans:2 * chans] = v.astype(jnp.bfloat16)
        left = jnp.where(col == 0, 0.0, pltpu.roll(v, 1, 0))
        right = jnp.where(col == cols - 1, 0.0, pltpu.roll(v, cols - 1, 0))
        act[e, r, :, 0:chans] = left.astype(jnp.bfloat16)
        act[e, r, :, 2 * chans:3 * chans] = right.astype(jnp.bfloat16)

    def activate_inside(e):
        def step(r, carry):
            activate(e, r)
            return carry
        lax.fori_loop(1, rows + 1, step, 0)
        activate(e, outer)

    def taps(f, a):
        total = None
        for b in range(3):
            window = act[f + a, b:b + rows].reshape(pix, 3 * chans)
            term = jnp.dot(window, cw[a, b], preferred_element_type=jnp.float32)
            total = term if total is None else total + term
        return total

    own_load.wait()
    activate_inside(2)
    activate_inside(3)
    row(2).wait()
    activate(2, inner)
    row(3).wait()
    activate(3, inner)
    w_loads[2].wait()
    acc[0] = taps(0, 2)
    acc[1] = taps(1, 2)
    w_loads[1].wait()
    acc[1] += taps(1, 1)

    def arrive(e):
        @pl.when(me >= 1)
        def _():
            halo(e).wait_recv()
            row(e).start()
        activate_inside(e)

        @pl.when(me >= 1)
        def _():
            row(e).wait()
        activate(e, inner)

    def copy_to(idx_src, idx_dst, q, by, send_sem):
        cut = pl.ds(q * chunk, chunk)
        return pltpu.make_async_remote_copy(
            src_ref=nb.at[idx_src, cut], dst_ref=nb.at[idx_dst, cut],
            send_sem=send_sem, recv_sem=nb_recv.at[idx_dst, q],
            device_id=peer(by), device_id_type=MESH)

    def own_next(f, q):
        return copy_to(8 + f, 6 + f, q, 1, own_send.at[0, f, q])

    def own_skip(f, q):
        return copy_to(8 + f, 4 + f, q, 2, own_send.at[1, f, q])

    def finish(f):
        mixed = raw[2 + f, 1:rows + 1].reshape(pix, chans).astype(jnp.float32) + acc[f]
        hidden = mixed.astype(jnp.bfloat16)
        held[f] = hidden
        nb[8 + f] = normalize(hidden.astype(jnp.float32)).astype(jnp.bfloat16)

        @pl.when(me <= n - 3)
        def _():
            for q in range(parts):
                own_skip(f, q).start()

        @pl.when(even)
        def _():
            for q in range(parts):
                own_next(f, q).start()

    arrive(1)
    w_loads[0].wait()
    acc[1] += taps(1, 0)
    finish(1)
    acc[0] += taps(0, 1)
    arrive(0)
    acc[0] += taps(0, 0)
    finish(0)

    for load in p_loads:
        load.wait()

    def keyed(idx):
        x = nb[idx]
        ks[idx] = jnp.dot(x, pw[1], preferred_element_type=jnp.float32).astype(jnp.bfloat16)
        vs[idx] = jnp.dot(x, pw[2], preferred_element_type=jnp.float32).astype(jnp.bfloat16)

    for f in (1, 0):
        qs[f] = jnp.dot(nb[8 + f], pw[0], preferred_element_type=jnp.float32).astype(jnp.bfloat16)
        keyed(8 + f)

    def fwd_side_even(f, q):
        return copy_to(4 + f, 2 + f, q, 1, fwd_send.at[0, f, q])

    def fwd_side_odd(f, q):
        return copy_to(4 + f, 6 + f, q, -1, fwd_send.at[0, f, q])

    def fwd_skip(f, q):
        return copy_to(4 + f, f, q, 2, fwd_send.at[1, f, q])

    def fwd_far_odd(f, q):
        return copy_to(f, 2 + f, q, -1, fwd_send.at[2, f, q])

    def landed(idx, q):
        copy_to(idx, idx, q, 0, own_send.at[0, 0, 0]).wait_recv()

    for f in (1, 0):
        for q in range(parts):
            @pl.when(even & (me >= 2))
            def _(f=f, q=q):
                landed(4 + f, q)
                fwd_side_even(f, q).start()

            if f == 1:
                @pl.when(even & (me >= 2) & (me <= n - 3))
                def _(f=f, q=q):
                    fwd_skip(f, q).start()

            @pl.when(odd & (me >= 2))
            def _(f=f, q=q):
                landed(4 + f, q)
                fwd_side_odd(f, q).start()

            @pl.when(odd & (me >= 2) & (me <= n - 3))
            def _(f=f, q=q):
                fwd_skip(f, q).start()
        keyed(4 + f)

    for f in (1, 0):
        for q in range(parts):
            @pl.when(odd & (me >= 4))
            def _(f=f, q=q):
                landed(f, q)
                fwd_far_odd(f, q).start()

            if f == 1:
                @pl.when(even & (me >= 4))
                def _(f=f, q=q):
                    landed(f, q)
        if f == 1:
            keyed(1)

    for d in (1, 3):
        for f in (1, 0):
            @pl.when(me >= d)
            def _(d=d, f=f):
                for q in range(parts):
                    landed(8 - 2 * d + f, q)
            keyed(8 - 2 * d + f)

    frames = ids.shape[0]
    lane = lax.broadcasted_iota(jnp.int32, (1, 128), 1)
    slot = lane // 8
    which = lax.rem(lane, 8) // 4
    first = me * 2
    local_first = first
    key_id = jnp.zeros((1, 128), jnp.int32)
    for s in range(9):
        at = lax.rem(local_first - REACH + s + frames, frames)
        key_id = jnp.where(slot == s, ids[at], key_id)
    query_id = jnp.where(which == 0, ids[local_first], ids[local_first + 1])
    key_frame = first - REACH + slot
    allowed = ((slot < 9) & (key_frame >= 0) & (key_frame <= first + which)
               & (slot >= which) & (slot < which + 8) & (key_id >= query_id - 1))

    scores = jnp.zeros((pix, 128), jnp.float32)
    for f in range(2):
        query = qs[f].astype(jnp.float32)
        for j in range(8):
            prod = query * ks[1 + f + j].astype(jnp.float32)
            high = prod.astype(jnp.bfloat16)
            low = (prod - high.astype(jnp.float32)).astype(jnp.bfloat16)
            spot = place[f * 8 + j]
            scores = scores + jnp.dot(high, spot, preferred_element_type=jnp.float32)
            scores = scores + jnp.dot(low, spot, preferred_element_type=jnp.float32)
    scores = jnp.where(allowed, scores, -1e30)
    top = scores
    for by in (64, 32, 16, 8):
        top = jnp.maximum(top, pltpu.roll(top, by, 1))
    expo = jnp.exp(scores - top)
    total = expo
    for by in (64, 32, 16, 8):
        total = total + pltpu.roll(total, by, 1)
    weights = (expo / total).astype(jnp.bfloat16)
    for f in range(2):
        got = jnp.zeros((pix, chans), jnp.float32)
        for j in range(8):
            wide = jnp.dot(weights, spread[f * 8 + j], preferred_element_type=jnp.float32)
            got = got + wide * vs[1 + f + j].astype(jnp.float32)
        mixed = held[f].astype(jnp.float32) + jnp.dot(
            got.astype(jnp.bfloat16), pw[3], preferred_element_type=jnp.float32)
        out[f] = mixed.astype(jnp.bfloat16).reshape(rows, cols, chans)

    @pl.when(me <= n - 2)
    def _():
        halo(1).wait_send()
        halo(0).wait_send()

    for f in range(2):
        for q in range(parts):
            @pl.when(me <= n - 3)
            def _(f=f, q=q):
                own_skip(f, q).wait_send()

            @pl.when(even)
            def _(f=f, q=q):
                own_next(f, q).wait_send()

            @pl.when(me >= 2)
            def _(f=f, q=q):
                fwd_side_even(f, q).wait_send()

            if f == 1:
                @pl.when(even & (me >= 2) & (me <= n - 3))
                def _(f=f, q=q):
                    fwd_skip(f, q).wait_send()

            @pl.when(odd & (me >= 2) & (me <= n - 3))
            def _(f=f, q=q):
                fwd_skip(f, q).wait_send()

            @pl.when(odd & (me >= 4))
            def _(f=f, q=q):
                fwd_far_odd(f, q).wait_send()


def per_device(video, block_ids, conv_weight, w_query, w_key, w_value, w_output):
    count, rows, cols, chans = video.shape
    n = lax.axis_size("tm")
    assert count == 2 and n % 2 == 0 and n >= 4 and lax.axis_size("height") == 2
    pix = rows * cols
    parts = 2
    bf = jnp.bfloat16
    anywhere = pl.BlockSpec(memory_space=pl.ANY)
    return pl.pallas_call(
        functools.partial(kernel, n, parts),
        out_shape=jax.ShapeDtypeStruct(video.shape, bf),
        in_specs=[pl.BlockSpec(memory_space=pltpu.SMEM)] + [anywhere] * 6,
        out_specs=pl.BlockSpec(memory_space=pltpu.VMEM),
        scratch_shapes=[
            pltpu.VMEM((4, rows + 2, cols, chans), bf),
            pltpu.VMEM((4, rows + 2, cols, 3 * chans), bf),
            pltpu.VMEM((3, 3, 3 * chans, chans), bf),
            pltpu.VMEM((4, chans, chans), bf),
            pltpu.VMEM((2, pix, chans), jnp.float32),
            pltpu.VMEM((2, pix, chans), bf),
            pltpu.VMEM((10, pix, chans), bf),
            pltpu.VMEM((2, pix, chans), bf),
            pltpu.VMEM((10, pix, chans), bf),
            pltpu.VMEM((10, pix, chans), bf),
            pltpu.VMEM((16, chans, 128), bf),
            pltpu.VMEM((16, 128, chans), bf),
            pltpu.SemaphoreType.DMA,
            pltpu.SemaphoreType.DMA((7,)),
            pltpu.SemaphoreType.DMA((4,)),
            pltpu.SemaphoreType.DMA((4,)),
            pltpu.SemaphoreType.DMA((2,)),
            pltpu.SemaphoreType.DMA((2,)),
            pltpu.SemaphoreType.DMA((2, 2, parts)),
            pltpu.SemaphoreType.DMA((3, 2, parts)),
            pltpu.SemaphoreType.DMA((10, parts)),
        ],
        compiler_params=pltpu.CompilerParams(collective_id=0, has_side_effects=True),
    )(block_ids, video, conv_weight.reshape(3, 3, 3 * chans, chans), w_query, w_key, w_value, w_output)


def solution(mesh):
    placed = (P(("groups", "tm"), "height", None, None), P("groups"), P(), P(), P(), P(), P())
    return jax.shard_map(
        per_device,
        mesh=mesh,
        in_specs=placed,
        out_specs=P(("groups", "tm"), "height", None, None),
        check_vma=False,
    )
```

time: 62.7 us -> 32.1 us (0.51)
  the two profiles are of different devices: /device:TPU:0 before, /device:TPU:16 now
where the time goes in v1:
time: 32.1 us; the launch traced here: 32 us
  Pallas kernels  30.3 us (94%)
  local copies, waits for them, and re-layouts  1.67 us (5%)
    pallas_call x1, Pallas kernels, per_device(): pl.pallas_call(functools.partial(kernel, n, parts), out_shape=jax.ShapeDt...  30.3 us
    unnamed x1, local copies, waits for them, and re-layouts  1.67 us

profile of v1, /device:TPU:16, one launch (start us, length us, event | category | flops | bytes accessed | tf_op | source)
XLA Modules:
  0.0 32.0 jit_solution(6408663625900619256)
XLA Ops:
  0.0 30.3 %shard_map.73 = bf16[2,4,64,256]{3,2,1,0:T(8,128)(2,1)} custom-call(s32[16]{0:T(128)} %ids.1, bf16[2,4,64,256]{3,2,1,0:T(8,128)(2,1)} %video.1, bf16[3,3,768,256]{3,2,1,0:T(8,128)(2,1)} %bitcast.1, bf16[256,256]{1,0:T(8,128)(2,1)} %w_q.1, bf16[256,256]{1,0:T(8,128)(2,1)} %w_k.1, bf16[256,256]{1,0:T(8,128)(2,1)} %w_v.1, bf16[256,256]{1,0:T(8,128)(2,1)} %w_o.1), custom_call_target="tpu_custom_call" | custom-call | tf_op jit(solution)/shard_map/pallas_call | solution.py:362
  30.3 1.7 %copy.9 = bf16[2,4,64,256]{3,2,1,0:T(8,128)(2,1)} copy(bf16[2,4,64,256]{3,2,1,0:T(8,128)(2,1)} %shard_map.73) | data formatting | bytes 524288

commit v2 on v0

v2 whole, which is shorter than its diff:
```python
import functools

import jax
import jax.numpy as jnp
from jax import lax
from jax.experimental import pallas as pl
from jax.experimental.pallas import tpu as pltpu
from jax.sharding import PartitionSpec as P

HD = 64
REACH = 7
MESH = pl.DeviceIdType.MESH


def normalize(wide):
    return wide * lax.rsqrt(jnp.mean(wide * wide, axis=-1, keepdims=True) + 1e-06)


def kernel(n, ids, video, conv_w, w_q, w_k, w_v, out, held,
           raw, act, cw, pw, acc, nb, qs, ks, vs, place, spread,
           load_sem, weight_sem, row_send, row_recv, halo_send, halo_recv,
           own_send, fwd_send, nb_recv):
    count, rows, cols, chans = video.shape
    me = lax.axis_index("tm")
    core = lax.axis_index("height")
    even = lax.rem(me, 2) == 0
    odd = lax.rem(me, 2) == 1

    def peer(by):
        return {"tm": me + by}

    other = {"height": 1 - core}

    own_load = pltpu.make_async_copy(video, raw.at[2:4, 1:rows + 1], load_sem)
    own_load.start()
    w_loads = {}
    for a in (2, 1, 0):
        w_loads[a] = pltpu.make_async_copy(conv_w.at[a], cw.at[a], weight_sem.at[a])
        w_loads[a].start()
    p_loads = []
    for j, w in enumerate((w_q, w_k, w_v)):
        p_loads.append(pltpu.make_async_copy(w, pw.at[j], weight_sem.at[3 + j]))
        p_loads[-1].start()

    barrier = pltpu.get_barrier_semaphore()
    near = [(me >= 1, -1), (me <= n - 2, 1), (me >= 2, -2), (me <= n - 3, 2)]
    pl.semaphore_signal(barrier, inc=1, device_id=other, device_id_type=MESH)
    for cond, by in near:
        @pl.when(cond)
        def _(by=by):
            pl.semaphore_signal(barrier, inc=1, device_id=peer(by), device_id_type=MESH)

    blank = jnp.zeros((cols, chans), jnp.bfloat16)
    outer = (rows + 1) * core
    inner = (rows + 1) * (1 - core)
    for e in range(4):
        raw[e, outer] = blank

    @pl.when(me == 0)
    def _():
        for e in range(2):
            for r in range(rows + 2):
                raw[e, r] = blank

    for d in range(1, 5):
        @pl.when(me < d)
        def _(d=d):
            for f in range(2):
                nb[8 - 2 * d + f] = jnp.zeros((rows, cols, chans), jnp.bfloat16)

    for at in (0, 1, n - 2, n - 1):
        @pl.when(me == at)
        def _(at=at):
            pl.semaphore_wait(barrier, 1 + sum(0 <= at + by < n for by in (-2, -1, 1, 2)))

    @pl.when((me >= 2) & (me <= n - 3))
    def _():
        pl.semaphore_wait(barrier, 5)

    edge = (rows - 1) * (1 - core)
    landing = (rows + 1) * core
    half = rows // 2

    def halo(part):
        start, size = ((core, rows - 1), (edge, 1))[part]
        return pltpu.make_async_remote_copy(
            src_ref=video.at[:, pl.ds(start, size)],
            dst_ref=raw.at[0:2, pl.ds(1 + start, size)],
            send_sem=halo_send.at[part], recv_sem=halo_recv.at[part],
            device_id=peer(1), device_id_type=MESH)

    def row(e):
        src = video.at[:, edge] if e else raw.at[0:2, 1 + edge]
        return pltpu.make_async_remote_copy(
            src_ref=src, dst_ref=raw.at[2 * e:2 * e + 2, landing],
            send_sem=row_send.at[e], recv_sem=row_recv.at[e],
            device_id=other, device_id_type=MESH)

    @pl.when(me <= n - 2)
    def _():
        halo(0).start()
        halo(1).start()

    row(1).start()

    col = lax.broadcasted_iota(jnp.int32, (cols, chans), 0)

    def activate(e, r):
        v = normalize(raw[e, r].astype(jnp.float32))
        v = v / (1.0 + jnp.exp(-v))
        act[e, r, :, chans:2 * chans] = v.astype(jnp.bfloat16)
        left = jnp.where(col == 0, 0.0, pltpu.roll(v, 1, 0))
        right = jnp.where(col == cols - 1, 0.0, pltpu.roll(v, cols - 1, 0))
        act[e, r, :, 0:chans] = left.astype(jnp.bfloat16)
        act[e, r, :, 2 * chans:3 * chans] = right.astype(jnp.bfloat16)

    def activate_rows(e0, start, size):
        for e in (e0, e0 + 1):
            for r in range(size):
                activate(e, start + r)

    empty = jnp.zeros((cols, 3 * chans), jnp.bfloat16)
    for e in range(4):
        act[e, outer] = empty

    def taps(p, a):
        base = half * (p + core * (1 - 2 * p))
        total = None
        for b in range(3):
            window = act[a:a + 2, pl.ds(base + b, half)].reshape(2 * half * cols, 3 * chans)
            term = jnp.dot(window, cw[a, b], preferred_element_type=jnp.float32)
            total = term if total is None else total + term
        return total

    own_load.wait()
    activate_rows(2, 1, rows)
    w_loads[2].wait()
    acc[0] = taps(0, 2)
    row(1).wait()
    activate_rows(2, inner, 1)
    acc[1] = taps(1, 2)
    w_loads[1].wait()
    w_loads[0].wait()

    def line(p):
        return p + core * (rows - 1 - 2 * p)

    def copy_to(src, dst, size, p, by, send_sem, recv_sem):
        return pltpu.make_async_remote_copy(
            src_ref=nb.at[src:src + size, line(p)], dst_ref=nb.at[dst:dst + size, line(p)],
            send_sem=send_sem, recv_sem=recv_sem,
            device_id=peer(by), device_id_type=MESH)

    def own_next(p):
        return copy_to(8, 6, 2, p, 1, own_send.at[0, p], nb_recv.at[0, p])

    def own_skip(p):
        return copy_to(8, 4, 2, p, 2, own_send.at[1, p], nb_recv.at[1, p])

    def fwd_side_even(p):
        return copy_to(4, 2, 2, p, 1, fwd_send.at[0, p], nb_recv.at[2, p])

    def fwd_side_odd(p):
        return copy_to(4, 6, 2, p, -1, fwd_send.at[0, p], nb_recv.at[0, p])

    def fwd_skip_even(p):
        return copy_to(5, 1, 1, p, 2, fwd_send.at[1, p], nb_recv.at[3, p])

    def fwd_skip_odd(p):
        return copy_to(4, 0, 2, p, 2, fwd_send.at[1, p], nb_recv.at[3, p])

    def fwd_far_odd(p):
        return copy_to(0, 2, 2, p, -1, fwd_send.at[2, p], nb_recv.at[2, p])

    def first_line(p):
        return half * (p + core * (1 - 2 * p))

    def finish(p):
        at = pl.ds(first_line(p), half)
        mixed = raw[2:4, pl.ds(first_line(p) + 1, half)].astype(jnp.float32)
        mixed = mixed + acc[p].reshape(mixed.shape)
        hidden = mixed.astype(jnp.bfloat16)
        held[:, at] = hidden
        nb[8:10, at] = normalize(hidden.astype(jnp.float32)).astype(jnp.bfloat16)
        for k in range(half):
            @pl.when(me <= n - 3)
            def _(k=k):
                own_skip(half * p + k).start()

            @pl.when(even)
            def _(k=k):
                own_next(half * p + k).start()

    @pl.when(me >= 1)
    def _():
        halo(0).wait_recv()
    activate_rows(0, 1 + core, rows - 1)
    acc[0] += taps(0, 1) + taps(0, 0)
    finish(0)

    @pl.when(me >= 1)
    def _():
        halo(1).wait_recv()
        row(0).start()
    activate_rows(0, 1 + edge, 1)

    @pl.when(me >= 1)
    def _():
        row(0).wait()
    activate_rows(0, inner, 1)
    acc[1] += taps(1, 1) + taps(1, 0)
    finish(1)

    c0 = lax.broadcasted_iota(jnp.int32, (chans, 128), 0) // HD
    l0 = lax.broadcasted_iota(jnp.int32, (chans, 128), 1)
    c1 = lax.broadcasted_iota(jnp.int32, (128, chans), 1) // HD
    l1 = lax.broadcasted_iota(jnp.int32, (128, chans), 0)
    for f in range(2):
        for s in range(f, f + 8):
            place[f * 8 + s - f] = jnp.where(
                l0 == c0 + (s * 8 + f * 4), HD ** (-0.5), 0.0).astype(jnp.bfloat16)
            spread[f * 8 + s - f] = jnp.where(
                l1 == c1 + (s * 8 + f * 4), 1.0, 0.0).astype(jnp.bfloat16)

    for load in p_loads:
        load.wait()

    def project(x, j):
        return jnp.dot(x, pw[j], preferred_element_type=jnp.float32).astype(jnp.bfloat16)

    def keyed(idx, size, p):
        at = pl.ds(first_line(p), half)
        shape = (size, half, cols, chans)
        x = nb[idx:idx + size, at].reshape(size * half * cols, chans)
        ks[idx:idx + size, at] = project(x, 1).reshape(shape)
        vs[idx:idx + size, at] = project(x, 2).reshape(shape)

    for p in range(2):
        at = pl.ds(first_line(p), half)
        x = nb[8:10, at].reshape(2 * half * cols, chans)
        qs[:, at] = project(x, 0).reshape(2, half, cols, chans)
        keyed(8, 2, p)

    def relay_near(p):
        @pl.when(even & (me >= 2))
        def _():
            own_skip(p).wait_recv()
            fwd_side_even(p).start()

        @pl.when(even & (me >= 2) & (me <= n - 3))
        def _():
            fwd_skip_even(p).start()

        @pl.when(odd & (me >= 2))
        def _():
            own_skip(p).wait_recv()
            fwd_side_odd(p).start()

        @pl.when(odd & (me >= 2) & (me <= n - 3))
        def _():
            fwd_skip_odd(p).start()

    def relay_far(p):
        @pl.when(odd & (me >= 4))
        def _():
            fwd_skip_odd(p).wait_recv()
            fwd_far_odd(p).start()

        @pl.when(even & (me >= 4))
        def _():
            fwd_skip_even(p).wait_recv()

    frames = ids.shape[0]
    lane = lax.broadcasted_iota(jnp.int32, (1, 128), 1)
    slot = lane // 8
    which = lax.rem(lane, 8) // 4
    first = me * 2
    key_id = jnp.zeros((1, 128), jnp.int32)
    for s in range(9):
        key_id = jnp.where(slot == s, ids[lax.rem(first - REACH + s + frames, frames)], key_id)
    query_id = jnp.where(which == 0, ids[first], ids[first + 1])
    key_frame = first - REACH + slot
    allowed = ((slot < 9) & (key_frame >= 0) & (key_frame <= first + which)
               & (slot >= which) & (slot < which + 8) & (key_id >= query_id - 1))

    def attend(p):
        at = pl.ds(first_line(p), half)
        group = half * cols

        def part(ref, idx):
            return ref[idx, at].reshape(group, chans).astype(jnp.float32)

        scores = jnp.zeros((group, 128), jnp.float32)
        for f in range(2):
            query = part(qs, f)
            for j in range(8):
                prod = query * part(ks, 1 + f + j)
                high = prod.astype(jnp.bfloat16)
                low = (prod - high.astype(jnp.float32)).astype(jnp.bfloat16)
                spot = place[f * 8 + j]
                scores = scores + jnp.dot(high, spot, preferred_element_type=jnp.float32)
                scores = scores + jnp.dot(low, spot, preferred_element_type=jnp.float32)
        scores = jnp.where(allowed, scores, -1e30)
        top = scores
        for by in (64, 32, 16, 8):
            top = jnp.maximum(top, pltpu.roll(top, by, 1))
        expo = jnp.exp(scores - top)
        total = expo
        for by in (64, 32, 16, 8):
            total = total + pltpu.roll(total, by, 1)
        weights = (expo / total).astype(jnp.bfloat16)
        for f in range(2):
            got = jnp.zeros((group, chans), jnp.float32)
            for j in range(8):
                wide = jnp.dot(weights, spread[f * 8 + j], preferred_element_type=jnp.float32)
                got = got + wide * part(vs, 1 + f + j)
            out[f, at] = got.astype(jnp.bfloat16).reshape(half, cols, chans)

    def take(d, p):
        sem = nb_recv.at[{1: 0, 3: 2}[d], p]

        @pl.when(me >= d)
        def _():
            copy_to(8 - 2 * d, 8 - 2 * d, 2, p, 1, own_send.at[0, 0], sem).wait_recv()

    for p in range(half):
        relay_near(p)
    keyed(4, 2, 0)
    for p in range(half, rows):
        relay_near(p)
    keyed(4, 2, 1)
    for p in range(half):
        relay_far(p)
    keyed(1, 1, 0)
    for p in range(half):
        take(1, p)
    keyed(6, 2, 0)
    relay_far(half)
    for p in range(half):
        take(3, p)
    keyed(2, 2, 0)
    attend(0)
    for p in range(half + 1, rows):
        relay_far(p)
    keyed(1, 1, 1)
    for p in range(half, rows):
        take(1, p)
    keyed(6, 2, 1)
    for p in range(half, rows):
        take(3, p)
    keyed(2, 2, 1)
    attend(1)

    @pl.when(me <= n - 2)
    def _():
        halo(0).wait_send()
        halo(1).wait_send()

    for p in range(rows):
        @pl.when(me <= n - 3)
        def _(p=p):
            own_skip(p).wait_send()

        @pl.when(even)
        def _(p=p):
            own_next(p).wait_send()

        @pl.when(me >= 2)
        def _(p=p):
            fwd_side_even(p).wait_send()

        @pl.when(even & (me >= 2) & (me <= n - 3))
        def _(p=p):
            fwd_skip_even(p).wait_send()

        @pl.when(odd & (me >= 2) & (me <= n - 3))
        def _(p=p):
            fwd_skip_odd(p).wait_send()

        @pl.when(odd & (me >= 4))
        def _(p=p):
            fwd_far_odd(p).wait_send()


def per_device(video, block_ids, conv_weight, w_query, w_key, w_value, w_output):
    count, rows, cols, chans = video.shape
    n = lax.axis_size("tm")
    assert count == 2 and n % 2 == 0 and n >= 4 and lax.axis_size("height") == 2
    assert rows % 2 == 0
    group = rows * cols
    bf = jnp.bfloat16
    anywhere = pl.BlockSpec(memory_space=pl.ANY)
    attended, hidden = pl.pallas_call(
        functools.partial(kernel, n),
        out_shape=[jax.ShapeDtypeStruct(video.shape, bf)] * 2,
        in_specs=[pl.BlockSpec(memory_space=pltpu.SMEM)] + [anywhere] * 5,
        out_specs=[pl.BlockSpec(memory_space=pltpu.VMEM)] * 2,
        scratch_shapes=[
            pltpu.VMEM((4, rows + 2, cols, chans), bf),
            pltpu.VMEM((4, rows + 2, cols, 3 * chans), bf),
            pltpu.VMEM((3, 3, 3 * chans, chans), bf),
            pltpu.VMEM((3, chans, chans), bf),
            pltpu.VMEM((2, group, chans), jnp.float32),
            pltpu.VMEM((10, rows, cols, chans), bf),
            pltpu.VMEM((2, rows, cols, chans), bf),
            pltpu.VMEM((10, rows, cols, chans), bf),
            pltpu.VMEM((10, rows, cols, chans), bf),
            pltpu.VMEM((16, chans, 128), bf),
            pltpu.VMEM((16, 128, chans), bf),
            pltpu.SemaphoreType.DMA,
            pltpu.SemaphoreType.DMA((6,)),
            pltpu.SemaphoreType.DMA((2,)),
            pltpu.SemaphoreType.DMA((2,)),
            pltpu.SemaphoreType.DMA((2,)),
            pltpu.SemaphoreType.DMA((2,)),
            pltpu.SemaphoreType.DMA((2, rows)),
            pltpu.SemaphoreType.DMA((3, rows)),
            pltpu.SemaphoreType.DMA((4, rows)),
        ],
        compiler_params=pltpu.CompilerParams(collective_id=0, has_side_effects=True),
    )(block_ids, video, conv_weight.reshape(3, 3, 3 * chans, chans), w_query, w_key, w_value)
    mixed = hidden.astype(jnp.float32).reshape(-1, chans) + jnp.dot(
        attended.reshape(-1, chans), w_output, preferred_element_type=jnp.float32)
    return mixed.astype(bf).reshape(video.shape)


def solution(mesh):
    placed = (P(("groups", "tm"), "height", None, None), P("groups"), P(), P(), P(), P(), P())
    return jax.shard_map(
        per_device,
        mesh=mesh,
        in_specs=placed,
        out_specs=P(("groups", "tm"), "height", None, None),
        check_vma=False,
    )
```

time: 62.7 us -> 32.6 us (0.52)
  the two profiles are of different devices: /device:TPU:0 before, /device:TPU:16 now
where the time goes in v2:
time: 32.6 us; the launch traced here: 32.4 us
  Pallas kernels  30.5 us (94%)
  matrix products  1.96 us (6%)
    pallas_call x1, Pallas kernels, per_device(): pl.pallas_call(functools.partial(kernel, n), out_shape=[jax.ShapeDtypeStr...  30.5 us
    dot_general x1, matrix products, per_device(): jnp.dot(attended.reshape(-1, chans), w_output, preferred_element_type=jnp...  1.96 us

profile of v2, /device:TPU:16, one launch (start us, length us, event | category | flops | bytes accessed | tf_op | source)
XLA Modules:
  0.0 32.4 jit_solution(15739787090497131405)
XLA Ops:
  0.0 0.0 copy-start
  0.0 30.5 %shard_map.73 = (bf16[2,4,64,256]{3,2,1,0:T(8,128)(2,1)}, bf16[2,4,64,256]{3,2,1,0:T(8,128)(2,1)}) custom-call(s32[16]{0:T(128)} %ids.1, bf16[2,4,64,256]{3,2,1,0:T(8,128)(2,1)} %video.1, bf16[3,3,768,256]{3,2,1,0:T(8,128)(2,1)} %bitcast.7, bf16[256,256]{1,0:T(8,128)(2,1)} %w_q.1, bf16[256,256]{1,0:T(8,128)(2,1)} %w_k.1, bf16[256,256]{1,0:T(8,128)(2,1)} %w_v.1), custom_call_target="tpu_custom_call" | custom-call | tf_op jit(solution)/shard_map/pallas_call | solution.py:393
  30.5 0.0 copy-done
  30.5 2.0 %fusion = bf16[512,256]{1,0:T(8,128)(2,1)} fusion(bf16[512,256]{1,0:T(8,128)(2,1)} %bitcast.8, bf16[256,256]{1,0:T(8,128)(2,1)S(1)} %copy-done, bf16[512,256]{1,0:T(8,128)(2,1)} %bitcast.9), kind=kOutput, calls=%fused_computation.1 | convolution fusion | flops 67502080 | bytes 917504 | tf_op jit(solution)/shard_map/dot_general | solution.py:422
Async XLA Ops:
  0.0 30.5 %copy-start = (bf16[256,256]{1,0:T(8,128)(2,1)S(1)}, bf16[256,256]{1,0:T(8,128)(2,1)}, u32[]{:S(2)}) copy-start(bf16[256,256]{1,0:T(8,128)(2,1)} %param.13) | copy-start | bytes 393220

commit v3 on v2

--- a/solution.py
+++ b/solution.py
@@ -191,26 +191,6 @@
             def _(k=k):
                 own_next(half * p + k).start()
 
-    @pl.when(me >= 1)
-    def _():
-        halo(0).wait_recv()
-    activate_rows(0, 1 + core, rows - 1)
-    acc[0] += taps(0, 1) + taps(0, 0)
-    finish(0)
-
-    @pl.when(me >= 1)
-    def _():
-        halo(1).wait_recv()
-        row(0).start()
-    activate_rows(0, 1 + edge, 1)
-
-    @pl.when(me >= 1)
-    def _():
-        row(0).wait()
-    activate_rows(0, inner, 1)
-    acc[1] += taps(1, 1) + taps(1, 0)
-    finish(1)
-
     c0 = lax.broadcasted_iota(jnp.int32, (chans, 128), 0) // HD
     l0 = lax.broadcasted_iota(jnp.int32, (chans, 128), 1)
     c1 = lax.broadcasted_iota(jnp.int32, (128, chans), 1) // HD
@@ -222,6 +202,26 @@
             spread[f * 8 + s - f] = jnp.where(
                 l1 == c1 + (s * 8 + f * 4), 1.0, 0.0).astype(jnp.bfloat16)
 
+    @pl.when(me >= 1)
+    def _():
+        halo(0).wait_recv()
+    activate_rows(0, 1 + core, rows - 1)
+    acc[0] += taps(0, 1) + taps(0, 0)
+    finish(0)
+
+    @pl.when(me >= 1)
+    def _():
+        halo(1).wait_recv()
+        row(0).start()
+    activate_rows(0, 1 + edge, 1)
+
+    @pl.when(me >= 1)
+    def _():
+        row(0).wait()
+    activate_rows(0, inner, 1)
+    acc[1] += taps(1, 1) + taps(1, 0)
+    finish(1)
+
     for load in p_loads:
         load.wait()
 
@@ -235,7 +235,7 @@
         ks[idx:idx + size, at] = project(x, 1).reshape(shape)
         vs[idx:idx + size, at] = project(x, 2).reshape(shape)
 
-    for p in range(2):
+    def own(p):
         at = pl.ds(first_line(p), half)
         x = nb[8:10, at].reshape(2 * half * cols, chans)
         qs[:, at] = project(x, 0).reshape(2, half, cols, chans)
@@ -323,31 +323,30 @@
         def _():
             copy_to(8 - 2 * d, 8 - 2 * d, 2, p, 1, own_send.at[0, 0], sem).wait_recv()
 
-    for p in range(half):
-        relay_near(p)
+    halves = (range(half), range(half, rows))
+    for h in range(2):
+        for p in halves[h]:
+            relay_near(p)
+        own(h)
     keyed(4, 2, 0)
-    for p in range(half, rows):
-        relay_near(p)
+    for p in halves[0]:
+        relay_far(p)
     keyed(4, 2, 1)
-    for p in range(half):
-        relay_far(p)
     keyed(1, 1, 0)
-    for p in range(half):
+    for p in halves[0]:
         take(1, p)
     keyed(6, 2, 0)
-    relay_far(half)
-    for p in range(half):
+    for p in halves[1]:
+        relay_far(p)
+    keyed(1, 1, 1)
+    for p in halves[0]:
         take(3, p)
     keyed(2, 2, 0)
     attend(0)
-    for p in range(half + 1, rows):
-        relay_far(p)
-    keyed(1, 1, 1)
-    for p in range(half, rows):
+    for p in halves[1]:
         take(1, p)
+        take(3, p)
     keyed(6, 2, 1)
-    for p in range(half, rows):
-        take(3, p)
     keyed(2, 2, 1)
     attend(1)
 

time: 32.6 us -> 32.1 us (0.985)
  Pallas kernels: 30.5 us -> 29.9 us
    pallas_call x1, Pallas kernels: 30.5 us -> 29.9 us  [per_device(): pl.pallas_call(functools.partial(kernel, n), out_shape=[jax.ShapeDtypeStr...]
where the time goes in v3:
time: 32.1 us; the launch traced here: 31.9 us
  Pallas kernels  29.9 us (93%)
  matrix products  1.96 us (6%)
    pallas_call x1, Pallas kernels, per_device(): pl.pallas_call(functools.partial(kernel, n), out_shape=[jax.ShapeDtypeStr...  29.9 us
    dot_general x1, matrix products, per_device(): jnp.dot(attended.reshape(-1, chans), w_output, preferred_element_type=jnp...  1.96 us

profile of v3, /device:TPU:16, one launch (start us, length us, event | category | flops | bytes accessed | tf_op | source)
XLA Modules:
  0.0 31.9 jit_solution(16296261209124321607)
XLA Ops:
  0.0 0.0 copy-start
  0.0 29.9 %shard_map.73 = (bf16[2,4,64,256]{3,2,1,0:T(8,128)(2,1)}, bf16[2,4,64,256]{3,2,1,0:T(8,128)(2,1)}) custom-call(s32[16]{0:T(128)} %ids.1, bf16[2,4,64,256]{3,2,1,0:T(8,128)(2,1)} %video.1, bf16[3,3,768,256]{3,2,1,0:T(8,128)(2,1)} %bitcast.7, bf16[256,256]{1,0:T(8,128)(2,1)} %w_q.1, bf16[256,256]{1,0:T(8,128)(2,1)} %w_k.1, bf16[256,256]{1,0:T(8,128)(2,1)} %w_v.1), custom_call_target="tpu_custom_call" | custom-call | tf_op jit(solution)/shard_map/pallas_call | solution.py:392
  29.9 0.0 copy-done
  30.0 2.0 %fusion = bf16[512,256]{1,0:T(8,128)(2,1)} fusion(bf16[512,256]{1,0:T(8,128)(2,1)} %bitcast.8, bf16[256,256]{1,0:T(8,128)(2,1)S(1)} %copy-done, bf16[512,256]{1,0:T(8,128)(2,1)} %bitcast.9), kind=kOutput, calls=%fused_computation.1 | convolution fusion | flops 67502080 | bytes 917504 | tf_op jit(solution)/shard_map/dot_general | solution.py:421
Async XLA Ops:
  0.0 29.9 %copy-start = (bf16[256,256]{1,0:T(8,128)(2,1)S(1)}, bf16[256,256]{1,0:T(8,128)(2,1)}, u32[]{:S(2)}) copy-start(bf16[256,256]{1,0:T(8,128)(2,1)} %param.13) | copy-start | bytes 393220
